TPU v7x, 128 devices: a whole 4x4x4 slice. The times are simulated.
128 devices in a mesh: dp: 8 (over z, core), mp: 16 (over y, x).
Axes of the slice: x: 4, y: 4, z: 4, core: 2. Of those that a mesh axis runs over, the one named last changes fastest.
Arguments:
- acts: bfloat16 [1024, 8192], P('dp', 'mp'), may hold values from -6 to 6
- w_up: bfloat16 [8192, 14336], P(None, 'mp'), may hold values from -0.0625 to 0.0625
- out_grad: bfloat16 [1024, 14336], P('dp', 'mp'), may hold values from -6 to 6
- rotation: float32 [8192, 8192], P('mp', 'dp'), may hold values from -6 to 6
Outputs:
- half_rotation: float32 [8192, 8192], P('mp', 'dp')
- next_rotation: float32 [8192, 8192], P('mp', 'dp')
All inputs are finite; a program needn't handle non-finite values.
Results may differ from a plain program's by a relative error of at most 0.017.
Values may be sent and summed in bfloat16 or wider, within the bound.
A program may use at most 128 MiB of HBM per device.

v0:
```python
import functools
import math
import jax
import jax.numpy as jnp
from jax import lax
from jax.sharding import Mesh
from jax.sharding import PartitionSpec as P

D = 8192
ITERS = 2
DP = ("dp_0", "dp_1")
MP = ("mp_0", "mp_1")
DP_MP = ("dp_0", "dp_1", "mp_0", "mp_1")
step_gain = 0.5
epsilon = 1e-06


def by_axis(value, axes):
    return functools.reduce(lax.psum, axes, value)


def in_one_piece(arrays, axis, dim, along):
    both = jnp.concatenate(arrays, axis=along)
    filled, at, gathered = (lax.all_gather(both, axis, axis=dim, tiled=True), 0, [])
    for a in arrays:
        gathered.append(lax.slice_in_dim(filled, at, at + a.shape[along], axis=along))
        at += a.shape[along]
    return tuple(gathered)


def settle(term):
    return lax.optimization_barrier(term.astype(jnp.bfloat16)).astype(jnp.float32)


def contract_cols(left, right):
    return lax.dot_general(
        left, right, (((1,), (1,)), ((), ())), preferred_element_type=jnp.float32
    )


def local(acts, w_up, out_grad, rotation):
    inv_root = D ** (-0.5)
    rot_half = rotation.astype(jnp.bfloat16)
    rot_rows = lax.all_gather(rot_half, DP, axis=1, tiled=True)
    mixed = lax.psum(
        (jnp.dot(acts, rot_rows, preferred_element_type=jnp.float32) * inv_root).astype(
            jnp.bfloat16
        ),
        MP,
    )
    hidden = jnp.dot(mixed, w_up, preferred_element_type=jnp.float32)
    sigmoid_hidden = jax.nn.sigmoid(hidden)
    grad_hidden = (
        out_grad.astype(jnp.float32) * sigmoid_hidden * (1.0 + hidden * (1.0 - sigmoid_hidden))
    ).astype(jnp.bfloat16)
    grad_mixed = lax.psum(contract_cols(grad_hidden, w_up).astype(jnp.bfloat16), MP)
    factor = contract_cols(grad_mixed, rot_rows).astype(jnp.bfloat16)
    act_norm, factor_norm = (
        by_axis(jnp.sum(jnp.square(acts.astype(jnp.float32))), DP_MP),
        by_axis(jnp.sum(jnp.square(factor.astype(jnp.float32))), DP_MP),
    )
    token_count = acts.shape[0] * lax.axis_size(DP)
    spread = (token_count ** (-0.5) + D ** (-0.5)) ** 2
    step_size = (
        step_gain
        * math.sqrt(D)
        / (jnp.sqrt((act_norm + epsilon) * (factor_norm + epsilon)) * spread)
    )
    every_acts, every_factor = in_one_piece((acts, factor), DP, 0, 1)
    groups = lax.axis_size(DP)
    block_rows = acts.shape[0]
    acts_blocks = every_acts.reshape(groups, block_rows, -1)
    factor_blocks = every_factor.reshape(groups, block_rows, -1)
    current = rotation
    first_iterate = rotation
    for iteration in range(ITERS):
        point = (rotation + current).astype(jnp.bfloat16)
        left_sum, right_sum = (
            lax.psum(
                (
                    jnp.dot(every_factor, point, preferred_element_type=jnp.float32) * inv_root
                ).astype(jnp.bfloat16),
                MP,
            ).astype(jnp.float32),
            lax.psum(
                (jnp.dot(every_acts, point, preferred_element_type=jnp.float32) * inv_root).astype(
                    jnp.bfloat16
                ),
                MP,
            ).astype(jnp.float32),
        )
        left = left_sum.astype(jnp.bfloat16).reshape(groups, block_rows, -1)
        right = right_sum.astype(jnp.bfloat16).reshape(groups, block_rows, -1)
        terms = jnp.einsum(
            "ntr,ntc->nrc", acts_blocks, left, preferred_element_type=jnp.float32
        ) - jnp.einsum("ntr,ntc->nrc", factor_blocks, right, preferred_element_type=jnp.float32)
        update = jnp.sum(settle(terms), axis=0)
        current = rotation - step_size * update
        if iteration == 0:
            first_iterate = current
    return (first_iterate, current)


def solution(mesh):
    finer = Mesh(mesh.devices.reshape(4, 2, 4, 4), ("dp_0", "dp_1", "mp_0", "mp_1"))
    placed = (P(DP, MP), P(None, MP), P(DP, MP), P(MP, DP))
    return jax.shard_map(
        local, mesh=finer, in_specs=placed, out_specs=(P(MP, DP), P(MP, DP)), check_vma=False
    )
```

profile of v0, /device:TPU:1, one launch (start us, length us, event | category | flops | bytes accessed | tf_op | source)
XLA Modules:
  0.0 586.6 jit_solution(2937792211861183039)
XLA Ops:
  7.2 0.0 copy-start.7
  7.2 0.0 all-gather.3.cloned.1.call-start
  7.2 2.8 convert_element_type.64
  10.0 0.0 all-gather.3.cloned.1.call-update
  10.0 0.0 all-reduce.11.cloned.1.call-start
  10.0 53.8 %all-gather.3.cloned.1.call-done = bf16[512,8192]{1,0:T(8,128)(2,1)} async-done(((bf16[512,1024]{1,0:T(8,128)(2,1)}), bf16[512,8192]{1,0:T(8,128)(2,1)}) %all-gather.3.cloned.1.call-update) | async-done | bytes 8388624 | tf_op jit(solution)/shard_map/all_gather | solution.py:44
  63.8 0.0 copy-done.7
  63.8 6.0 %fusion = bf16[128,8192]{1,0:T(8,128)(2,1)} fusion(bf16[128,512]{1,0:T(8,128)(2,1)S(1)} %copy-done.7, bf16[512,8192]{1,0:T(8,128)(2,1)} %all-gather.3.cloned.1.call-done), kind=kOutput, calls=%fused_computation.5 | convolution fusion | flops 1075838976 | bytes 10616832 | tf_op jit(solution)/shard_map/dot_general | solution.py:46
  69.9 0.0 copy-start.8
  69.9 0.0 all-reduce.11.cloned.1.call-update
  69.9 0.0 all-reduce.13.cloned.1.call-start
  69.9 88.7 %all-reduce.11.cloned.1.call-done = bf16[128,8192]{1,0:T(8,128)(2,1)} async-done(((bf16[128,8192]{1,0:T(8,128)(2,1)}), bf16[128,8192]{1,0:T(8,128)(2,1)}) %all-reduce.11.cloned.1.call-update) | async-done | bytes 2097168 | tf_op jit(solution)/shard_map/psum | solution.py:45
  158.6 0.0 copy-done.8
  158.6 20.2 %convolution_convert_fusion = bf16[128,8192]{1,0:T(8,128)(2,1)} fusion(bf16[8192,896]{1,0:T(8,128)(2,1)} %param.5, bf16[128,896]{1,0:T(8,128)(2,1)S(1)} %copy-done.8, bf16[128,8192]{1,0:T(8,128)(2,1)} %all-reduce.11.cloned.1.call-done), kind=kOutput, calls=%fused_computation.6 | convolution fusion | flops 3760291840 | bytes 19103744 | tf_op jit(solution)/shard_map/dot_general | solution.py:36
  178.8 0.0 all-reduce.13.cloned.1.call-update
  178.8 0.0 copy-start
  178.8 0.0 all-gather.5.cloned.1.call-start
  178.9 89.5 %all-reduce.13.cloned.1.call-done = bf16[128,8192]{1,0:T(8,128)(2,1)} async-done(((bf16[128,8192]{1,0:T(8,128)(2,1)}), bf16[128,8192]{1,0:T(8,128)(2,1)}) %all-reduce.13.cloned.1.call-update) | async-done | bytes 2097168 | tf_op jit(solution)/shard_map/psum | solution.py:56
  268.4 7.7 %multiply_reduce_fusion = (f32[]{:T(128)}, bf16[128,512]{1,0:T(8,128)(2,1)S(1)}) fusion(bf16[128,8192]{1,0:T(8,128)(2,1)} %all-reduce.13.cloned.1.call-done, bf16[512,8192]{1,0:T(8,128)(2,1)} %all-gather.3.cloned.1.call-done), kind=kOutput, calls=%fused_computation.18 | convolution fusion | flops 1074003968 | bytes 10616836 | tf_op jit(solution)/shard_map/dot_general | solution.py:36
  276.1 0.7 pad_maximum_fusion
  276.8 0.0 all-gather.5.cloned.1.call-update
  276.8 0.0 all-reduce.17.cloned.1.call-start
  276.9 26.4 %all-gather.5.cloned.1.call-done = bf16[1024,1024]{1,0:T(8,128)(2,1)} async-done(((bf16[128,1024]{1,0:T(8,128)(2,1)}), bf16[1024,1024]{1,0:T(8,128)(2,1)}) %all-gather.5.cloned.1.call-update) | async-done | bytes 2097168 | tf_op jit(solution)/shard_map/all_gather | solution.py:24
  303.3 0.0 copy-done
  303.3 0.0 copy-start.5
  303.3 4.0 multiply_convert_fusion.3
  307.2 0.0 copy-done.5
  307.2 2.6 multiply_convert_fusion.2
  309.8 0.0 all-reduce.17.cloned.1.call-update
  309.8 0.0 all-reduce.15.cloned.1.call-start
  309.9 0.7 multiply_reduce_fusion.1
  310.6 7.9 %all-reduce.2 = (f32[]{:T(128)}, f32[]{:T(128)}) all-reduce(f32[]{:T(128)} %multiply_reduce_fusion.1, f32[]{:T(128)} %get-tuple-element.18), channel_id=1, replica_groups=mesh['dp_0'=4,'dp_1'=2,'mp_0'=4,'mp_1'=4] {'dp_0'}, use_global_device_ids=true, to_apply=%region_1.0 | all-reduce | flops 2 | bytes 16 | tf_op jit(solution)/shard_map/psum | solution.py:19
  318.5 5.1 all-reduce.3
  323.6 9.9 %all-reduce.1 = (f32[]{:T(128)}, f32[]{:T(128)}) all-reduce(f32[]{:T(128)} %get-tuple-element.8, f32[]{:T(128)} %get-tuple-element.9), channel_id=1, replica_groups=mesh['dp_0'=4,'dp_1'=2,'mp_0'=4,'mp_1'=4] {'mp_0'}, use_global_device_ids=true, to_apply=%region_3.0 | all-reduce | flops 2 | bytes 16 | tf_op jit(solution)/shard_map/psum | solution.py:19
  333.5 9.3 %all-reduce = (f32[]{:T(128)}, f32[]{:T(128)}) all-reduce(f32[]{:T(128)} %get-tuple-element.4, f32[]{:T(128)} %get-tuple-element.5), channel_id=1, replica_groups=mesh['dp_0'=4,'dp_1'=2,'mp_0'=4,'mp_1'=4] {'mp_1'}, use_global_device_ids=true, to_apply=%region_4.0 | all-reduce | flops 2 | bytes 16 | tf_op jit(solution)/shard_map/psum | solution.py:19
  344.2 2.6 fusion.7
  346.9 66.5 %all-reduce.17.cloned.1.call-done = (bf16[8,128,1024]{2,1,0:T(8,128)(2,1)}, bf16[8,128,1024]{2,1,0:T(8,128)(2,1)}) async-done(((bf16[8,128,1024]{2,1,0:T(8,128)(2,1)}, bf16[8,128,1024]{2,1,0:T(8,128)(2,1)}), (bf16[8,128,1024]{2,1,0:T(8,128)(2,1)}, bf16[8,128,1024]{2,1,0:T(8,128)(2,1)})) %all-reduce.17.cloned.1.call-update) | async-done | bytes 4194320 | tf_op jit(solution)/shard_map/psum | solution.py:79
  413.4 0.0 copy-start.1
  413.4 0.0 copy-start.3
  413.4 9.8 %fusion.10 = f32[8,512,1024]{2,1,0:T(8,128)} fusion(bf16[8,128,512]{2,1,0:T(8,128)(2,1)S(1)} %bitcast.23, bf16[8,128,1024]{2,1,0:T(8,128)(2,1)} %get-tuple-element.12), kind=kOutput, calls=%fused_computation.28 | convolution fusion | flops 1073741824 | bytes 19922944 | tf_op jit(solution)/shard_map/ntr,ntc->nrc/dot_general | solution.py:94
  423.2 0.0 copy-done.1
  423.2 0.0 copy-done.3
  423.2 11.4 %subtract_convert_fusion.1 = bf16[8,512,1024]{2,1,0:T(8,128)(2,1)} fusion(f32[8,512,1024]{2,1,0:T(8,128)} %fusion.10, bf16[8,128,512]{2,1,0:T(8,128)(2,1)S(1)} %bitcast.25, bf16[8,128,1024]{2,1,0:T(8,128)(2,1)S(1)} %copy-done.3), kind=kOutput, calls=%fused_computation.3 | convolution fusion | flops 1082130432 | bytes 28311552 | tf_op jit(solution)/shard_map/ntr,ntc->nrc/dot_general | solution.py:96
  434.6 5.7 convert_reduce_fusion.1
  440.3 0.0 copy-start.6
  440.3 1.8 add_convert_fusion
  442.2 0.0 copy-done.6
  442.2 2.6 multiply_convert_fusion
  444.8 2.6 multiply_convert_fusion.1
  447.4 0.0 all-reduce.15.cloned.1.call-update
  447.4 103.4 %all-reduce.15.cloned.1.call-done = (bf16[8,128,1024]{2,1,0:T(8,128)(2,1)}, bf16[8,128,1024]{2,1,0:T(8,128)(2,1)}) async-done(((bf16[8,128,1024]{2,1,0:T(8,128)(2,1)}, bf16[8,128,1024]{2,1,0:T(8,128)(2,1)}), (bf16[8,128,1024]{2,1,0:T(8,128)(2,1)}, bf16[8,128,1024]{2,1,0:T(8,128)(2,1)})) %all-reduce.15.cloned.1.call-update) | async-done | bytes 4194320 | tf_op jit(solution)/shard_map/psum | solution.py:79
  550.8 0.0 copy-start.2
  550.8 0.0 copy-start.4
  550.8 9.8 %fusion.11 = f32[8,512,1024]{2,1,0:T(8,128)} fusion(bf16[8,128,512]{2,1,0:T(8,128)(2,1)S(1)} %bitcast.24, bf16[8,128,1024]{2,1,0:T(8,128)(2,1)} %get-tuple-element.10), kind=kOutput, calls=%fused_computation.29 | convolution fusion | flops 1073741824 | bytes 19922944 | tf_op jit(solution)/shard_map/ntr,ntc->nrc/dot_general | solution.py:94
  560.6 0.0 copy-done.2
  560.7 0.0 copy-done.4
  560.7 11.7 %subtract_convert_fusion = bf16[8,512,1024]{2,1,0:T(8,128)(2,1)} fusion(f32[8,512,1024]{2,1,0:T(8,128)} %fusion.11, bf16[8,128,512]{2,1,0:T(8,128)(2,1)S(1)} %bitcast.26, bf16[8,128,1024]{2,1,0:T(8,128)(2,1)S(1)} %copy-done.4), kind=kOutput, calls=%fused_computation.1 | convolution fusion | flops 1082130432 | bytes 28311552 | tf_op jit(solution)/shard_map/ntr,ntc->nrc/dot_general | solution.py:96
  572.3 5.7 convert_reduce_fusion
  578.0 1.8 multiply_subtract_fusion
Async XLA Ops:
  7.2 56.7 %copy-start.7 = (bf16[128,512]{1,0:T(8,128)(2,1)S(1)}, bf16[128,512]{1,0:T(8,128)(2,1)}, u32[]{:S(2)}) copy-start(bf16[128,512]{1,0:T(8,128)(2,1)} %param.4) | copy-start | bytes 393220
  7.2 56.7 %all-gather.3.cloned.1.call-start = ((), (), s32[]{:S(2)}) async-start(), calls=%async_computation | async-start | bytes 9437184 | tf_op jit(solution)/shard_map/all_gather | solution.py:44
  10.0 148.6 %all-reduce.11.cloned.1.call-start = ((), (), s32[]{:S(2)}) async-start(), calls=%async_computation.1 | async-start | bytes 4194304 | tf_op jit(solution)/shard_map/psum | solution.py:45
  69.9 88.8 %copy-start.8 = (bf16[128,896]{1,0:T(8,128)(2,1)S(1)}, bf16[128,896]{1,0:T(8,128)(2,1)}, u32[]{:S(2)}) copy-start(bf16[128,896]{1,0:T(8,128)(2,1)} %param.6) | copy-start | bytes 688132
  69.9 198.5 %all-reduce.13.cloned.1.call-start = ((), (), s32[]{:S(2)}) async-start(), calls=%async_computation.2 | async-start | bytes 4194304 | tf_op jit(solution)/shard_map/psum | solution.py:56
  178.8 124.4 %copy-start = (f32[512,1024]{1,0:T(8,128)S(1)}, f32[512,1024]{1,0:T(8,128)}, u32[]{:S(2)}) copy-start(f32[512,1024]{1,0:T(8,128)} %param.7) | copy-start | bytes 6291460
  178.8 124.4 %all-gather.5.cloned.1.call-start = ((), (), s32[]{:S(2)}) async-start(), calls=%async_computation.3 | async-start | bytes 2359296 | tf_op jit(solution)/shard_map/all_gather | solution.py:24
  276.8 136.5 %all-reduce.17.cloned.1.call-start = ((), (), s32[]{:S(2)}) async-start(), calls=%async_computation.5 | async-start | bytes 8388608 | tf_op jit(solution)/shard_map/psum | solution.py:79
  303.3 4.0 copy-start.5
  309.8 241.0 %all-reduce.15.cloned.1.call-start = ((), (), s32[]{:S(2)}) async-start(), calls=%async_computation.4 | async-start | bytes 8388608 | tf_op jit(solution)/shard_map/psum | solution.py:79
  413.4 9.8 %copy-start.1 = (bf16[1024,512]{1,0:T(8,128)(2,1)S(1)}, bf16[1024,512]{1,0:T(8,128)(2,1)}, u32[]{:S(2)}) copy-start(bf16[1024,512]{1,0:T(8,128)(2,1)} %get-tuple-element.16) | copy-start | bytes 3145732
  413.4 9.8 %copy-start.3 = (bf16[8,128,1024]{2,1,0:T(8,128)(2,1)S(1)}, bf16[8,128,1024]{2,1,0:T(8,128)(2,1)}, u32[]{:S(2)}) copy-start(bf16[8,128,1024]{2,1,0:T(8,128)(2,1)} %get-tuple-element.13) | copy-start | bytes 6291460
  440.3 1.9 copy-start.6
  550.8 9.8 %copy-start.2 = (bf16[1024,512]{1,0:T(8,128)(2,1)S(1)}, bf16[1024,512]{1,0:T(8,128)(2,1)}, u32[]{:S(2)}) copy-start(bf16[1024,512]{1,0:T(8,128)(2,1)} %get-tuple-element.16) | copy-start | bytes 3145732
  550.8 9.8 %copy-start.4 = (bf16[8,128,1024]{2,1,0:T(8,128)(2,1)S(1)}, bf16[8,128,1024]{2,1,0:T(8,128)(2,1)}, u32[]{:S(2)}) copy-start(bf16[8,128,1024]{2,1,0:T(8,128)(2,1)} %get-tuple-element.11) | copy-start | bytes 6291460
Sparse Core Ops, SparseCore 0:
  10.3 53.5 all-gather.2
  70.0 88.5 all-reduce.10
  178.9 89.4 all-reduce.12
  276.9 26.2 all-gather.4
  310.0 103.3 all-reduce.16
  447.5 103.2 all-reduce.14
where the time goes:
time: 587 us
  waiting for transfers between devices  428 us (73%)
  matrix products  88.4 us (15%)
  blocking collectives  32.2 us (5%)
  other arithmetic  19.1 us (3%)
  between operations  15.6 us (3%)
    psum x2, waiting for transfers between devices, local(): lax.psum((jnp.dot(every_factor, point, preferred_element_type=jnp.float32...  170 us
    psum x1, waiting for transfers between devices, local(): lax.psum(contract_cols(grad_hidden, w_up).astype(jnp.bfloat16), MP)  89.5 us
    psum x1, waiting for transfers between devices, local(): lax.psum((jnp.dot(acts, rot_rows, preferred_element_type=jnp.float32) * i...  88.7 us
    all_gather x1, waiting for transfers between devices, local(): rot_rows = lax.all_gather(rot_half, DP, axis=1, tiled=True)  53.8 us
    psum x4, blocking collectives, by_axis(): return functools.reduce(lax.psum, axes, value)  32.2 us
    dot_general x2, matrix products, contract_cols(): lax.dot_general(left, right, (((1,), (1,)), ((), ())), preferred_element_...  27.8 us
    all_gather x1, waiting for transfers between devices, in_one_piece(): lax.all_gather(both, axis, axis=dim, tiled=True)  26.4 us
    dot_general x2, matrix products, local(): jnp.einsum('ntr,ntc->nrc', factor_blocks, right, preferred_element_type=j...  23.1 us
  transfers between devices with their start and end apart: 6, of which 6 were waited for; matrix products, arithmetic and copies ran while one was open for 1% of the time, Pallas kernels for 0%

commit v1 on v0

--- a/solution.py
+++ b/solution.py
@@ -53,7 +53,9 @@
     grad_hidden = (
         out_grad.astype(jnp.float32) * sigmoid_hidden * (1.0 + hidden * (1.0 - sigmoid_hidden))
     ).astype(jnp.bfloat16)
-    grad_mixed = lax.psum(contract_cols(grad_hidden, w_up).astype(jnp.bfloat16), MP)
+    grad_mixed = lax.psum(
+        lax.psum(contract_cols(grad_hidden, w_up).astype(jnp.bfloat16), "mp_1"), "mp_0"
+    )
     factor = contract_cols(grad_mixed, rot_rows).astype(jnp.bfloat16)
     act_norm, factor_norm = (
         by_axis(jnp.sum(jnp.square(acts.astype(jnp.float32))), DP_MP),

time: 587 us -> 617 us (1.051)
  waiting for transfers between devices: 428 us -> 458 us
    psum x1 -> x2, waiting for transfers between devices: 89.5 us -> 120 us  [the longest x1 60.7 us: local(): lax.psum(lax.psum(contract_cols(grad_hidden, w_up).astype(jnp.bfloat16),...]
  transfers between devices with their start and end apart: 6 -> 7, of which waited for: 6 -> 7; matrix products, arithmetic and copies ran while one was open for 1% -> 1% of each run, Pallas kernels for 0% -> 0%
where the time goes in v1:
time: 617 us; the launch traced here: 616 us
  waiting for transfers between devices  458 us (74%)
  matrix products  88.4 us (14%)
  blocking collectives  32.2 us (5%)
  other arithmetic  19.1 us (3%)
  between operations  15.6 us (3%)
    psum x2, waiting for transfers between devices, local(): lax.psum((jnp.dot(every_factor, point, preferred_element_type=jnp.float32...  170 us
    psum x1, waiting for transfers between devices, local(): lax.psum((jnp.dot(acts, rot_rows, preferred_element_type=jnp.float32) * i...  88.7 us
    psum x1, waiting for transfers between devices, local(): lax.psum(lax.psum(contract_cols(grad_hidden, w_up).astype(jnp.bfloat16),...  60.7 us
    psum x1, waiting for transfers between devices, local(): lax.psum(contract_cols(grad_hidden, w_up).astype(jnp.bfloat16), 'mp_1')  59.3 us
    all_gather x1, waiting for transfers between devices, local(): rot_rows = lax.all_gather(rot_half, DP, axis=1, tiled=True)  53.8 us
    psum x4, blocking collectives, by_axis(): return functools.reduce(lax.psum, axes, value)  32.2 us
    dot_general x2, matrix products, contract_cols(): lax.dot_general(left, right, (((1,), (1,)), ((), ())), preferred_element_...  27.8 us
    all_gather x1, waiting for transfers between devices, in_one_piece(): lax.all_gather(both, axis, axis=dim, tiled=True)  25.7 us
  transfers between devices with their start and end apart: 7, of which 7 were waited for; matrix products, arithmetic and copies ran while one was open for 1% of the time, Pallas kernels for 0%

profile of v1, /device:TPU:1, one launch (start us, length us, event | category | flops | bytes accessed | tf_op | source)
XLA Modules:
  0.0 616.4 jit_solution(11206416425595151286)
XLA Ops:
  7.2 0.0 copy-start.7
  7.2 0.0 all-gather.3.cloned.1.call-start
  7.2 2.8 convert_element_type.64
  10.0 0.0 all-gather.3.cloned.1.call-update
  10.0 0.0 all-reduce.12.cloned.1.call-start
  10.0 53.8 %all-gather.3.cloned.1.call-done = bf16[512,8192]{1,0:T(8,128)(2,1)} async-done(((bf16[512,1024]{1,0:T(8,128)(2,1)}), bf16[512,8192]{1,0:T(8,128)(2,1)}) %all-gather.3.cloned.1.call-update) | async-done | bytes 8388624 | tf_op jit(solution)/shard_map/all_gather | solution.py:44
  63.8 0.0 copy-done.7
  63.8 6.0 fusion
  69.9 0.0 copy-start.8
  69.9 0.0 all-reduce.12.cloned.1.call-update
  69.9 0.0 all-reduce.14.cloned.1.call-start
  69.9 88.7 %all-reduce.12.cloned.1.call-done = bf16[128,8192]{1,0:T(8,128)(2,1)} async-done(((bf16[128,8192]{1,0:T(8,128)(2,1)}), bf16[128,8192]{1,0:T(8,128)(2,1)}) %all-reduce.12.cloned.1.call-update) | async-done | bytes 2097168 | tf_op jit(solution)/shard_map/psum | solution.py:45
  158.6 0.0 copy-done.8
  158.6 20.2 %convolution_convert_fusion = bf16[128,8192]{1,0:T(8,128)(2,1)} fusion(bf16[8192,896]{1,0:T(8,128)(2,1)} %param.5, bf16[128,896]{1,0:T(8,128)(2,1)S(1)} %copy-done.8, bf16[128,8192]{1,0:T(8,128)(2,1)} %all-reduce.12.cloned.1.call-done), kind=kOutput, calls=%fused_computation.6 | convolution fusion | flops 3760291840 | bytes 19103744 | tf_op jit(solution)/shard_map/dot_general | solution.py:36
  178.8 0.0 all-reduce.14.cloned.1.call-update
  178.8 0.0 all-reduce.16.cloned.1.call-start
  178.9 59.3 %all-reduce.14.cloned.1.call-done = bf16[128,8192]{1,0:T(8,128)(2,1)} async-done(((bf16[128,8192]{1,0:T(8,128)(2,1)}), bf16[128,8192]{1,0:T(8,128)(2,1)}) %all-reduce.14.cloned.1.call-update) | async-done | bytes 2097168 | tf_op jit(solution)/shard_map/psum | solution.py:57
  238.1 0.0 all-reduce.16.cloned.1.call-update
  238.2 0.0 copy-start
  238.2 0.0 all-gather.5.cloned.1.call-start
  238.2 60.7 %all-reduce.16.cloned.1.call-done = bf16[128,8192]{1,0:T(8,128)(2,1)} async-done(((bf16[128,8192]{1,0:T(8,128)(2,1)}), bf16[128,8192]{1,0:T(8,128)(2,1)}) %all-reduce.16.cloned.1.call-update) | async-done | bytes 2097168 | tf_op jit(solution)/shard_map/psum | solution.py:56
  298.9 7.7 %multiply_reduce_fusion = (f32[]{:T(128)}, bf16[128,512]{1,0:T(8,128)(2,1)S(1)}) fusion(bf16[128,8192]{1,0:T(8,128)(2,1)} %all-reduce.16.cloned.1.call-done, bf16[512,8192]{1,0:T(8,128)(2,1)} %all-gather.3.cloned.1.call-done), kind=kOutput, calls=%fused_computation.18 | convolution fusion | flops 1074003968 | bytes 10616836 | tf_op jit(solution)/shard_map/dot_general | solution.py:36
  306.6 0.7 pad_maximum_fusion
  307.3 0.0 all-gather.5.cloned.1.call-update
  307.3 0.0 all-reduce.20.cloned.1.call-start
  307.4 25.7 %all-gather.5.cloned.1.call-done = bf16[1024,1024]{1,0:T(8,128)(2,1)} async-done(((bf16[128,1024]{1,0:T(8,128)(2,1)}), bf16[1024,1024]{1,0:T(8,128)(2,1)}) %all-gather.5.cloned.1.call-update) | async-done | bytes 2097168 | tf_op jit(solution)/shard_map/all_gather | solution.py:24
  333.0 0.0 copy-done
  333.0 0.0 copy-start.5
  333.0 4.0 multiply_convert_fusion.3
  337.0 0.0 copy-done.5
  337.0 2.6 multiply_convert_fusion.2
  339.6 0.0 all-reduce.20.cloned.1.call-update
  339.6 0.0 all-reduce.18.cloned.1.call-start
  339.7 0.7 multiply_reduce_fusion.1
  340.3 7.9 %all-reduce.2 = (f32[]{:T(128)}, f32[]{:T(128)}) all-reduce(f32[]{:T(128)} %multiply_reduce_fusion.1, f32[]{:T(128)} %get-tuple-element.18), channel_id=1, replica_groups=mesh['dp_0'=4,'dp_1'=2,'mp_0'=4,'mp_1'=4] {'dp_0'}, use_global_device_ids=true, to_apply=%region_1.0 | all-reduce | flops 2 | bytes 16 | tf_op jit(solution)/shard_map/psum | solution.py:19
  348.2 5.1 all-reduce.3
  353.3 9.9 %all-reduce.1 = (f32[]{:T(128)}, f32[]{:T(128)}) all-reduce(f32[]{:T(128)} %get-tuple-element.8, f32[]{:T(128)} %get-tuple-element.9), channel_id=1, replica_groups=mesh['dp_0'=4,'dp_1'=2,'mp_0'=4,'mp_1'=4] {'mp_0'}, use_global_device_ids=true, to_apply=%region_3.0 | all-reduce | flops 2 | bytes 16 | tf_op jit(solution)/shard_map/psum | solution.py:19
  363.2 9.3 %all-reduce = (f32[]{:T(128)}, f32[]{:T(128)}) all-reduce(f32[]{:T(128)} %get-tuple-element.4, f32[]{:T(128)} %get-tuple-element.5), channel_id=1, replica_groups=mesh['dp_0'=4,'dp_1'=2,'mp_0'=4,'mp_1'=4] {'mp_1'}, use_global_device_ids=true, to_apply=%region_4.0 | all-reduce | flops 2 | bytes 16 | tf_op jit(solution)/shard_map/psum | solution.py:19
  374.0 2.6 fusion.7
  376.7 66.5 %all-reduce.20.cloned.1.call-done = (bf16[8,128,1024]{2,1,0:T(8,128)(2,1)}, bf16[8,128,1024]{2,1,0:T(8,128)(2,1)}) async-done(((bf16[8,128,1024]{2,1,0:T(8,128)(2,1)}, bf16[8,128,1024]{2,1,0:T(8,128)(2,1)}), (bf16[8,128,1024]{2,1,0:T(8,128)(2,1)}, bf16[8,128,1024]{2,1,0:T(8,128)(2,1)})) %all-reduce.20.cloned.1.call-update) | async-done | bytes 4194320 | tf_op jit(solution)/shard_map/psum | solution.py:81
  443.1 0.0 copy-start.1
  443.1 0.0 copy-start.3
  443.1 9.8 %fusion.10 = f32[8,512,1024]{2,1,0:T(8,128)} fusion(bf16[8,128,512]{2,1,0:T(8,128)(2,1)S(1)} %bitcast.23, bf16[8,128,1024]{2,1,0:T(8,128)(2,1)} %get-tuple-element.12), kind=kOutput, calls=%fused_computation.28 | convolution fusion | flops 1073741824 | bytes 19922944 | tf_op jit(solution)/shard_map/ntr,ntc->nrc/dot_general | solution.py:96
  453.0 0.0 copy-done.1
  453.0 0.0 copy-done.3
  453.0 11.4 %subtract_convert_fusion.1 = bf16[8,512,1024]{2,1,0:T(8,128)(2,1)} fusion(f32[8,512,1024]{2,1,0:T(8,128)} %fusion.10, bf16[8,128,512]{2,1,0:T(8,128)(2,1)S(1)} %bitcast.25, bf16[8,128,1024]{2,1,0:T(8,128)(2,1)S(1)} %copy-done.3), kind=kOutput, calls=%fused_computation.3 | convolution fusion | flops 1082130432 | bytes 28311552 | tf_op jit(solution)/shard_map/ntr,ntc->nrc/dot_general | solution.py:98
  464.4 5.7 convert_reduce_fusion.1
  470.1 0.0 copy-start.6
  470.1 1.8 add_convert_fusion
  472.0 0.0 copy-done.6
  472.0 2.6 multiply_convert_fusion
  474.6 2.6 multiply_convert_fusion.1
  477.1 0.0 all-reduce.18.cloned.1.call-update
  477.2 103.4 %all-reduce.18.cloned.1.call-done = (bf16[8,128,1024]{2,1,0:T(8,128)(2,1)}, bf16[8,128,1024]{2,1,0:T(8,128)(2,1)}) async-done(((bf16[8,128,1024]{2,1,0:T(8,128)(2,1)}, bf16[8,128,1024]{2,1,0:T(8,128)(2,1)}), (bf16[8,128,1024]{2,1,0:T(8,128)(2,1)}, bf16[8,128,1024]{2,1,0:T(8,128)(2,1)})) %all-reduce.18.cloned.1.call-update) | async-done | bytes 4194320 | tf_op jit(solution)/shard_map/psum | solution.py:81
  580.6 0.0 copy-start.2
  580.6 0.0 copy-start.4
  580.6 9.8 %fusion.11 = f32[8,512,1024]{2,1,0:T(8,128)} fusion(bf16[8,128,512]{2,1,0:T(8,128)(2,1)S(1)} %bitcast.24, bf16[8,128,1024]{2,1,0:T(8,128)(2,1)} %get-tuple-element.10), kind=kOutput, calls=%fused_computation.29 | convolution fusion | flops 1073741824 | bytes 19922944 | tf_op jit(solution)/shard_map/ntr,ntc->nrc/dot_general | solution.py:96
  590.5 0.0 copy-done.2
  590.5 0.0 copy-done.4
  590.5 11.7 %subtract_convert_fusion = bf16[8,512,1024]{2,1,0:T(8,128)(2,1)} fusion(f32[8,512,1024]{2,1,0:T(8,128)} %fusion.11, bf16[8,128,512]{2,1,0:T(8,128)(2,1)S(1)} %bitcast.26, bf16[8,128,1024]{2,1,0:T(8,128)(2,1)S(1)} %copy-done.4), kind=kOutput, calls=%fused_computation.1 | convolution fusion | flops 1082130432 | bytes 28311552 | tf_op jit(solution)/shard_map/ntr,ntc->nrc/dot_general | solution.py:98
  602.2 5.7 convert_reduce_fusion
  607.8 1.8 multiply_subtract_fusion
Async XLA Ops:
  7.2 56.7 %copy-start.7 = (bf16[128,512]{1,0:T(8,128)(2,1)S(1)}, bf16[128,512]{1,0:T(8,128)(2,1)}, u32[]{:S(2)}) copy-start(bf16[128,512]{1,0:T(8,128)(2,1)} %param.4) | copy-start | bytes 393220
  7.2 56.7 %all-gather.3.cloned.1.call-start = ((), (), s32[]{:S(2)}) async-start(), calls=%async_computation | async-start | bytes 9437184 | tf_op jit(solution)/shard_map/all_gather | solution.py:44
  10.0 148.6 %all-reduce.12.cloned.1.call-start = ((), (), s32[]{:S(2)}) async-start(), calls=%async_computation.1 | async-start | bytes 4194304 | tf_op jit(solution)/shard_map/psum | solution.py:45
  69.9 88.8 %copy-start.8 = (bf16[128,896]{1,0:T(8,128)(2,1)S(1)}, bf16[128,896]{1,0:T(8,128)(2,1)}, u32[]{:S(2)}) copy-start(bf16[128,896]{1,0:T(8,128)(2,1)} %param.6) | copy-start | bytes 688132
  69.9 168.3 %all-reduce.14.cloned.1.call-start = ((), (), s32[]{:S(2)}) async-start(), calls=%async_computation.2 | async-start | bytes 4194304 | tf_op jit(solution)/shard_map/psum | solution.py:57
  178.8 120.1 %all-reduce.16.cloned.1.call-start = ((), (), s32[]{:S(2)}) async-start(), calls=%async_computation.3 | async-start | bytes 4194304 | tf_op jit(solution)/shard_map/psum | solution.py:56
  238.2 94.9 %copy-start = (f32[512,1024]{1,0:T(8,128)S(1)}, f32[512,1024]{1,0:T(8,128)}, u32[]{:S(2)}) copy-start(f32[512,1024]{1,0:T(8,128)} %param.7) | copy-start | bytes 6291460
  238.2 94.9 %all-gather.5.cloned.1.call-start = ((), (), s32[]{:S(2)}) async-start(), calls=%async_computation.4 | async-start | bytes 2359296 | tf_op jit(solution)/shard_map/all_gather | solution.py:24
  307.3 135.8 %all-reduce.20.cloned.1.call-start = ((), (), s32[]{:S(2)}) async-start(), calls=%async_computation.6 | async-start | bytes 8388608 | tf_op jit(solution)/shard_map/psum | solution.py:81
  333.0 4.0 copy-start.5
  339.6 241.0 %all-reduce.18.cloned.1.call-start = ((), (), s32[]{:S(2)}) async-start(), calls=%async_computation.5 | async-start | bytes 8388608 | tf_op jit(solution)/shard_map/psum | solution.py:81
  443.1 9.8 %copy-start.1 = (bf16[1024,512]{1,0:T(8,128)(2,1)S(1)}, bf16[1024,512]{1,0:T(8,128)(2,1)}, u32[]{:S(2)}) copy-start(bf16[1024,512]{1,0:T(8,128)(2,1)} %get-tuple-element.16) | copy-start | bytes 3145732
  443.1 9.8 %copy-start.3 = (bf16[8,128,1024]{2,1,0:T(8,128)(2,1)S(1)}, bf16[8,128,1024]{2,1,0:T(8,128)(2,1)}, u32[]{:S(2)}) copy-start(bf16[8,128,1024]{2,1,0:T(8,128)(2,1)} %get-tuple-element.13) | copy-start | bytes 6291460
  470.1 1.9 copy-start.6
  580.6 9.8 %copy-start.2 = (bf16[1024,512]{1,0:T(8,128)(2,1)S(1)}, bf16[1024,512]{1,0:T(8,128)(2,1)}, u32[]{:S(2)}) copy-start(bf16[1024,512]{1,0:T(8,128)(2,1)} %get-tuple-element.16) | copy-start | bytes 3145732
  580.6 9.8 %copy-start.4 = (bf16[8,128,1024]{2,1,0:T(8,128)(2,1)S(1)}, bf16[8,128,1024]{2,1,0:T(8,128)(2,1)}, u32[]{:S(2)}) copy-start(bf16[8,128,1024]{2,1,0:T(8,128)(2,1)} %get-tuple-element.11) | copy-start | bytes 6291460
Sparse Core Ops, SparseCore 0:
  10.3 53.5 all-gather.2
  70.0 88.5 all-reduce.11
  178.9 59.1 all-reduce.13
  240.3 58.5 all-reduce.15
  307.4 25.5 all-gather.4
  339.7 103.3 all-reduce.19
  477.3 103.2 all-reduce.17
